TPU v7x, 512 devices: a whole 4x4x16 slice. The times are simulated.
512 devices in a mesh: leaf: 32 (over x, y, core), row: 16 (over z).
Axes of the slice: x: 4, y: 4, z: 16, core: 2. Of those that a mesh axis runs over, the one named last changes fastest.
Arguments:
- rhs: bfloat16 [32, 16, 189, 512], P('leaf', 'row'), may hold values from -6 to 6
- inv_diag: bfloat16 [32, 16, 189, 1536], P('leaf', 'row'), may hold values from -0.15625 to 0.15625
- off_diag: bfloat16 [32, 16, 96, 12384], P('leaf', 'row'), may hold values from -0.0390625 to 0.0390625
- pair_mask: int32 [32, 16, 15], P('leaf', 'row'), may hold values 0 or 1
Outputs:
- solution: float32 [32, 16, 189, 512], P('leaf', 'row')
All inputs are finite; a program needn't handle non-finite values. No bound on the sum of `pair_mask` on one device may be relied on, other than what follows from the above.
Results may differ from a plain program's by a relative error of at most 0.0065.
Values may be sent and summed in bfloat16 or wider, within the bound.
No kernel may reach another device: no remote copies, remote signals or barrier semaphores. Data moves between devices by JAX's collectives and lax.ppermute only.
A program may use at most 64 MiB of HBM per device.

v0:
```python
import jax
import jax.numpy as jnp
from jax import lax
from jax.sharding import PartitionSpec as P

F32 = jnp.float32
BF16 = jnp.bfloat16


def column_start(ancestor, source, width_all):
    offset = 0
    for higher in range(1, ancestor):
        for within in range(higher):
            offset += width_all // 2**within
    for within in range(source):
        offset += width_all // 2**within
    return offset


def dot(a, b):
    return jnp.dot(a, b, preferred_element_type=F32)


def dot_t(a, b):
    return lax.dot_general(a, b, (((1,), (b.ndim - 1,)), ((), ())), preferred_element_type=F32)


def core_swap(block):
    count = lax.axis_size("leaf")
    return lax.ppermute(block, "leaf", [(i, i ^ 1) for i in range(count)])


def leaf_groups(size):
    count = lax.axis_size("leaf")
    return [[first + i for i in range(size)] for first in range(0, count, size)]


def leaf_scatter(pieces):
    size = pieces.shape[0]
    return lax.all_to_all(pieces, "leaf", 0, 0, tiled=True, axis_index_groups=leaf_groups(size))


def leaf_everyone(block, size):
    return leaf_scatter(jnp.broadcast_to(block, (size, *block.shape)))


def shards(rhs, inv_diag, off_diag, pair_mask):
    rows_n = lax.axis_size("row")
    leaves = lax.axis_size("leaf")
    levels = leaves.bit_length() - 1
    width = inv_diag.shape[3]
    cols = rhs.shape[3]
    strip = width // rows_n
    half = cols // 2
    sub = half // rows_n
    leaf = lax.axis_index("leaf")
    core = leaf % 2
    first_core = core == 0
    b_all = rhs[0, 0]
    d_all = inv_diag[0, 0]
    panels = off_diag[0, 0]
    live = pair_mask[0, 0]
    heights = [strip >> m for m in range(levels + 1)]
    starts = [sum(heights[:m]) for m in range(levels + 1)]

    def panel(m, l):
        first = column_start(m, l, width)
        return panels[:, first : first + (width >> l)]

    def alive(m, l, dtype):
        return live[m * (m - 1) // 2 + l].astype(dtype)

    def masked(m, l):
        return panel(m, l) * alive(m, l, BF16)

    d_own0 = d_all[: heights[0]]
    d_full0 = lax.all_gather(d_own0, "row", axis=0, tiled=True)
    b0 = b_all[: heights[0]]
    z0 = jnp.concatenate(
        [
            lax.all_gather(b0[:, :half], "row", axis=0, tiled=True),
            lax.all_gather(b0[:, half:], "row", axis=0, tiled=True),
        ],
        axis=1,
    )
    d_own1 = d_all[starts[1] : starts[2]]
    mid = width // 2
    own1 = jnp.concatenate(
        [masked(m, 1) for m in range(2, levels + 1)] + [d_own1[:, :mid], d_own1[:, mid:]], axis=0
    )
    other1 = core_swap(own1)
    p_rows = strip * (levels - 1)
    p_own1 = own1[:p_rows]
    p_other1 = other1[:p_rows]
    d_other1 = jnp.concatenate(
        [other1[p_rows : p_rows + heights[1]], other1[p_rows + heights[1] :]], axis=1
    )
    upper_pairs = sorted(
        ((m, l) for l in range(2, levels) for m in range(l + 1, levels + 1)),
        key=lambda p: (p[1], p[0]),
    )
    d_up = d_all[starts[2] :]
    d_rows = d_up.shape[0]
    d_pad = strip // 2
    d_up = jnp.concatenate([d_up, jnp.zeros((d_pad - d_rows, width), BF16)], axis=0)
    packed = jnp.concatenate(
        [jnp.concatenate([d_up[:, :mid], d_up[:, mid:]], axis=0)]
        + [masked(m, l) for m, l in upper_pairs],
        axis=1,
    )
    packed, d_full0 = lax.optimization_barrier((packed, d_full0))
    everyone = lax.all_gather(packed, "row", axis=0, tiled=False)
    yb0 = dot(d_full0, z0).astype(BF16)
    out0 = dot(d_own0, z0)
    parts = []
    for m in range(1, levels + 1):
        placed = lax.dynamic_update_slice(
            jnp.zeros((strip, cols), BF16),
            b_all[starts[m] : starts[m] + heights[m]],
            (leaf % 2**m * heights[m], 0),
        )
        parts.append(placed.astype(F32) - dot(panel(m, 0), yb0) * alive(m, 0, F32))
    part = jnp.concatenate(parts, axis=0)
    kept = jnp.where(first_core, part[:, :half], part[:, half:])
    sent = jnp.where(first_core, part[:, half:], part[:, :half]).astype(BF16)
    part = kept + core_swap(sent).astype(F32)

    def natural1(block):
        pieces = lax.all_gather(block, "row", axis=0, tiled=False)
        return (
            pieces.reshape(rows_n, 2, heights[1], half).transpose(1, 0, 2, 3).reshape(2, mid, half)
        )

    z1 = natural1(part[:strip].astype(BF16)).reshape(width, half)
    y_own1 = dot(d_own1, z1)
    y_other1 = dot(d_other1, z1)
    yb1 = jnp.where(
        first_core,
        jnp.concatenate([y_own1, y_other1], axis=0),
        jnp.concatenate([y_other1, y_own1], axis=0),
    ).astype(BF16)
    y_got1 = core_swap(y_other1)
    out1 = jnp.where(
        first_core,
        jnp.concatenate([y_own1, y_got1], axis=1),
        jnp.concatenate([y_got1, y_own1], axis=1),
    )
    yn1 = natural1(yb1)
    here = jnp.where(first_core, yn1[0], yn1[1])
    there = jnp.where(first_core, yn1[1], yn1[0])
    part = part[strip:] - (dot(p_own1, here) + dot(p_other1, there))
    turned = part.T.astype(BF16).reshape(rows_n, sub, p_rows)
    turned = lax.all_to_all(turned, "row", 0, 0, tiled=True)

    def turned_of(m):
        return turned[:, :, (m - 2) * strip : (m - 1) * strip]

    def d_leaf(m):
        low = starts[m] - starts[2]
        left = everyone[:, low : low + heights[m], :mid]
        right = everyone[:, d_pad + low : d_pad + low + heights[m], :mid]
        return jnp.concatenate([left, right], axis=2).reshape(rows_n * heights[m], width)

    p_leaf = {}
    at = mid
    for m, l in upper_pairs:
        p_leaf[m, l] = everyone[:, :, at : at + (width >> l)]
        at += width >> l

    def natural(z, m):
        z = z.reshape(rows_n, 2 * sub, 2**m, heights[m])
        return z.transpose(1, 2, 0, 3).reshape(2 * sub, width)

    solved = []
    sums = {}
    for m in range(2, levels + 1):
        if m == 2:
            pieces = leaf_everyone(turned_of(2), 4).astype(F32)
            pieces = pieces.reshape(2, 2, rows_n, sub, strip).sum(axis=0).astype(BF16)
            z = pieces.transpose(1, 0, 2, 3).reshape(rows_n, 2 * sub, strip)
        else:
            size = 2**m
            mine = jnp.where(
                (jnp.arange(2) == core)[None, :, None, None],
                turned_of(m)[:, None],
                jnp.zeros((), BF16),
            ).reshape(rows_n, 2 * sub, strip)
            v = (mine.astype(F32) - sums[m]).astype(BF16)
            if size <= rows_n:
                v = v.reshape(size, rows_n // size, 2 * sub, strip)
                z = leaf_scatter(v).astype(F32).sum(axis=0).astype(BF16)
                z = leaf_everyone(z, size).reshape(rows_n, 2 * sub, strip)
            else:
                cut = size // rows_n
                v = v.reshape(rows_n, 2 * sub, cut, strip // cut).transpose(0, 2, 1, 3)
                v = v.reshape(size, 2 * sub, strip // cut)
                z = leaf_scatter(v).astype(F32).sum(axis=0).astype(BF16)
                z = leaf_everyone(z, size).reshape(rows_n, cut, 2 * sub, strip // cut)
                z = z.transpose(0, 2, 1, 3).reshape(rows_n, 2 * sub, strip)
        y = dot_t(natural(z, m), d_leaf(m))
        yb = y.astype(BF16)
        solved.append(yb.reshape(2 * sub, rows_n, heights[m]))
        for higher in range(m + 1, levels + 1):
            term = dot_t(yb, p_leaf[higher, m]).transpose(1, 0, 2)
            sums[higher] = term if m == 2 else sums[higher] + term
    done = jnp.concatenate(solved, axis=2).transpose(1, 0, 2)
    done = lax.all_to_all(done, "row", 0, 0, tiled=True)
    done = done.reshape(rows_n, 2, sub, d_rows).transpose(3, 1, 0, 2).reshape(d_rows, cols)
    return jnp.concatenate([out0, out1, done.astype(F32)], axis=0)[None, None]


def solution(mesh):
    in_specs = (
        P("leaf", "row", None, None),
        P("leaf", "row", None, None),
        P("leaf", "row", None, None),
        P("leaf", "row", None),
    )
    out_specs = P("leaf", "row", None, None)
    return jax.shard_map(shards, mesh=mesh, in_specs=in_specs, out_specs=out_specs, check_vma=False)
```

profile of v0, /device:TPU:1, one launch (start us, length us, event | category | flops | bytes accessed | tf_op | source)
XLA Modules:
  0.0 420.5 jit_solution(10371558072732546112)
XLA Ops:
  14.2 3.0 slice_multiply_fusion.4
  18.1 67.4 %all-gather.6.cloned.1.call-done = bf16[1,1,1536,1536]{3,2,1,0:T(8,128)(2,1)} async-done(((bf16[1,1,96,1536]{3,2,1,0:T(8,128)(2,1)}), bf16[1,1,1536,1536]{3,2,1,0:T(8,128)(2,1)}) %all-gather.6.cloned.1.call-update) | async-done | bytes 4718608 | tf_op jit(solution)/shard_map/all_gather | solution.py:77
  89.9 2.4 constant_dynamic-update-slice_fusion.3
  92.3 2.4 constant_dynamic-update-slice_fusion.2
  96.0 10.9 %collective-permute-start.1 = (bf16[480,768]{1,0:T(8,128)(2,1)}, bf16[480,768]{1,0:T(8,128)(2,1)S(1)}, u32[]{:S(2)}, u32[]{:S(2)}) collective-permute-start(bf16[480,768]{1,0:T(8,128)(2,1)} %slice_dynamic-update-slice_fusion), channel_id=1, source_target_pairs={{0,16},{16,0},{32,48},{48,32},{64,80},{80,64},{96,112},{112,96},{1... | collective-permute-start | bytes 2211848 | tf_op jit(solution)/shard_map/ppermute | solution.py:30
  111.7 37.0 %all_gather.25 = bf16[1536,256]{1,0:T(8,128)(2,1)S(1)} all-gather(bf16[96,256]{1,0:T(8,128)(2,1)S(1)} %get-tuple-element.43), channel_id=1, replica_groups=mesh['leaf'=32,'row'=16] {'row'}, dimensions={0}, use_global_device_ids=true | all-gather | bytes 835584 | tf_op jit(solution)/shard_map/all_gather | solution.py:81
  148.8 36.5 %all_gather.26 = bf16[1536,256]{1,0:T(8,128)(2,1)S(1)} all-gather(bf16[96,256]{1,0:T(8,128)(2,1)S(1)} %get-tuple-element.42), channel_id=1, replica_groups=mesh['leaf'=32,'row'=16] {'row'}, dimensions={0}, use_global_device_ids=true | all-gather | bytes 835584 | tf_op jit(solution)/shard_map/all_gather | solution.py:82
  185.4 2.6 convolution_convert_fusion
  190.1 9.7 %collective-permute-start = (bf16[480,256]{1,0:T(8,128)(2,1)S(1)}, bf16[480,256]{1,0:T(8,128)(2,1)S(1)}, u32[]{:S(2)}, u32[]{:S(2)}) collective-permute-start(bf16[480,256]{1,0:T(8,128)(2,1)S(1)} %select_convert_fusion), channel_id=1, source_target_pairs={{0,16},{16,0},{32,48},{48,32},{64,80},{80,64},{96,112},{112,96},{1... | collective-permute-start | bytes 737288 | tf_op jit(solution)/shard_map/ppermute | solution.py:30
  201.0 25.1 %all-gather.1 = bf16[1536,256]{1,0:T(8,128)(2,1)S(1)} all-gather(bf16[96,256]{1,0:T(8,128)(2,1)S(1)} %slice.485), channel_id=3, replica_groups=mesh['leaf'=32,'row'=16] {'row'}, dimensions={0}, use_global_device_ids=true | all-gather | bytes 835584 | tf_op jit(solution)/shard_map/all_gather | solution.py:129
  228.2 24.3 %all_gather.30 = bf16[16,96,256]{2,1,0:T(8,128)(2,1)S(1)} all-gather(bf16[1,96,256]{2,1,0:T(8,128)(2,1)S(1)} %fusion.61), channel_id=1, replica_groups=mesh['leaf'=32,'row'=16] {'row'}, dimensions={0}, use_global_device_ids=true | all-gather | bytes 835584 | tf_op jit(solution)/shard_map/all_gather | solution.py:129
  253.4 20.8 %all_to_all.45 = bf16[16,16,384]{2,1,0:T(8,128)(2,1)S(1)} all-to-all(bf16[16,16,384]{2,1,0:T(8,128)(2,1)S(1)} %bitcast.226), channel_id=1, replica_groups=mesh['leaf'=32,'row'=16] {'row'}, dimensions={0} | all-to-all | bytes 393216 | tf_op jit(solution)/shard_map/all_to_all | solution.py:153
  275.1 18.8 %all-to-all-start.1 = ((bf16[4,16,16,96]{3,2,1,0:T(8,128)(2,1)}), bf16[4,16,16,96]{3,2,1,0:T(8,128)(2,1)S(1)}, u32[]{:S(2)}, u32[]{:S(2)}) async-start(bf16[4,16,16,96]{3,2,1,0:T(8,128)(2,1)} %broadcast_in_dim.70), calls=%async_computation.1 | async-start | bytes 524288 | tf_op jit(solution)/shard_map/all_to_all | solution.py:40
  304.5 2.7 fusion.2
  307.2 2.6 fusion
  309.8 2.6 fusion.33
  312.4 5.2 %all-to-all-start.2 = ((bf16[8,2,32,96]{3,2,1,0:T(8,128)(2,1)}), bf16[8,2,32,96]{3,2,1,0:T(8,128)(2,1)S(1)}, u32[]{:S(2)}, u32[]{:S(2)}) async-start(bf16[8,2,32,96]{3,2,1,0:T(8,128)(2,1)} %bitcast.55), calls=%async_computation.2 | async-start | bytes 262144 | tf_op jit(solution)/shard_map/all_to_all | solution.py:40
  318.7 4.2 all-to-all-done.2
  323.6 4.7 %all-to-all-start.3 = ((bf16[8,2,32,96]{3,2,1,0:T(8,128)(2,1)}), bf16[8,2,32,96]{3,2,1,0:T(8,128)(2,1)}, u32[]{:S(2)}, u32[]{:S(2)}) async-start(bf16[8,2,32,96]{3,2,1,0:T(8,128)(2,1)} %broadcast_in_dim.77), calls=%async_computation.3 | async-start | bytes 262144 | tf_op jit(solution)/shard_map/all_to_all | solution.py:40
  330.5 3.2 all-to-all-done.3
  339.0 2.3 fusion.36
  341.3 4.3 %all-to-all-start.4 = ((bf16[16,1,32,96]{3,2,1,0:T(8,128)(2,1)}), bf16[16,1,32,96]{3,2,1,0:T(8,128)(2,1)S(1)}, u32[]{:S(2)}, u32[]{:S(2)}) async-start(bf16[16,1,32,96]{3,2,1,0:T(8,128)(2,1)} %fusion.36), calls=%async_computation.4 | async-start | bytes 262144 | tf_op jit(solution)/shard_map/all_to_all | solution.py:40
  346.8 4.9 %all-to-all-done.4 = bf16[16,1,32,96]{3,2,1,0:T(8,128)(2,1)S(1)} async-done(((bf16[16,1,32,96]{3,2,1,0:T(8,128)(2,1)}), bf16[16,1,32,96]{3,2,1,0:T(8,128)(2,1)S(1)}, u32[]{:S(2)}, u32[]{:S(2)}) %all-to-all-start.4) | async-done | bytes 98336 | tf_op jit(solution)/shard_map/all_to_all | solution.py:40
  352.4 4.0 all-to-all-start.5
  356.4 2.4 convolution_add_fusion.2
  358.8 3.8 all-to-all-done.5
  366.2 5.6 %all-to-all-start.6 = ((bf16[32,2,768]{2,1,0:T(2,128)(2,1)}), bf16[32,2,768]{2,1,0:T(2,128)(2,1)S(1)}, u32[]{:S(2)}, u32[]{:S(2)}) async-start(bf16[32,2,768]{2,1,0:T(2,128)(2,1)} %reshape.243), calls=%async_computation.6 | async-start | bytes 196608 | tf_op jit(solution)/shard_map/all_to_all | solution.py:40
  373.0 6.3 %all-to-all-done.6 = bf16[32,2,768]{2,1,0:T(2,128)(2,1)S(1)} async-done(((bf16[32,2,768]{2,1,0:T(2,128)(2,1)}), bf16[32,2,768]{2,1,0:T(2,128)(2,1)S(1)}, u32[]{:S(2)}, u32[]{:S(2)}) %all-to-all-start.6) | async-done | bytes 98336 | tf_op jit(solution)/shard_map/all_to_all | solution.py:40
  380.7 3.9 all-to-all-start.7
  386.0 6.1 %all-to-all-done.7 = bf16[32,2,768]{2,1,0:T(2,128)(2,1)S(1)} async-done(((bf16[32,2,768]{2,1,0:T(2,128)(2,1)}), bf16[32,2,768]{2,1,0:T(2,128)(2,1)S(1)}, u32[]{:S(2)}, u32[]{:S(2)}) %all-to-all-start.7) | async-done | bytes 98336 | tf_op jit(solution)/shard_map/all_to_all | solution.py:40
  395.8 4.8 %all-to-all-start.8 = ((bf16[16,2,720]{2,1,0:T(2,128)(2,1)}), bf16[16,2,720]{2,1,0:T(2,128)(2,1)S(1)}, u32[]{:S(2)}, u32[]{:S(2)}) async-start(bf16[16,2,720]{2,1,0:T(2,128)(2,1)} %reshape.247), calls=%async_computation.8 | async-start | bytes 98304 | tf_op jit(solution)/shard_map/all_to_all | solution.py:207
  401.9 10.3 %all-to-all-done.8 = bf16[16,2,720]{2,1,0:T(2,128)(2,1)S(1)} async-done(((bf16[16,2,720]{2,1,0:T(2,128)(2,1)}), bf16[16,2,720]{2,1,0:T(2,128)(2,1)S(1)}, u32[]{:S(2)}, u32[]{:S(2)}) %all-to-all-start.8) | async-done | bytes 46112 | tf_op jit(solution)/shard_map/all_to_all | solution.py:207
  (152 shorter events, 58.3 us)
Async XLA Ops:
  6.5 78.9 %all-gather.6.cloned.1.call-start = ((), (), s32[]{:S(2)}) async-start(), calls=%async_computation.9 | async-start | bytes 5013504 | tf_op jit(solution)/shard_map/all_gather | solution.py:77
  8.3 292.4 %all-gather.8.cloned.1.call-start = ((), (), s32[]{:S(2)}) async-start(), calls=%async_computation.10 | async-start | bytes 7938048 | tf_op jit(solution)/shard_map/all_gather | solution.py:112
  17.2 77.5 %copy-start.1 = (bf16[1,1,189,1536]{3,2,1,0:T(8,128)(2,1)S(1)}, bf16[1,1,189,1536]{3,2,1,0:T(8,128)(2,1)}, u32[]{:S(2)}) copy-start(bf16[1,1,189,1536]{3,2,1,0:T(8,128)(2,1)} %param.5) | copy-start | bytes 1741828
  18.1 88.8 %copy-start.13 = (s32[1,1,15]{2,1,0:T(1,128)S(1)}, s32[1,1,15]{2,1,0:T(1,128)}, u32[]{:S(2)}) copy-start(s32[1,1,15]{2,1,0:T(1,128)} %param.7) | copy-start | bytes 184
  18.1 92.8 %copy-start.9 = (bf16[1,1,189,512]{3,2,1,0:T(8,128)(2,1)S(1)}, bf16[1,1,189,512]{3,2,1,0:T(8,128)(2,1)}, u32[]{:S(2)}) copy-start(bf16[1,1,189,512]{3,2,1,0:T(8,128)(2,1)} %param.4) | copy-start | bytes 580612
  96.0 103.9 %collective-permute-start.1 = (bf16[480,768]{1,0:T(8,128)(2,1)}, bf16[480,768]{1,0:T(8,128)(2,1)S(1)}, u32[]{:S(2)}, u32[]{:S(2)}) collective-permute-start(bf16[480,768]{1,0:T(8,128)(2,1)} %slice_dynamic-update-slice_fusion), channel_id=1, source_target_pairs={{0,16},{16,0},{32,48},{48,32},{64,80},{80,64},{96,112},{112,96},{1... | collective-permute-start | bytes 2211848 | tf_op jit(solution)/shard_map/ppermute | solution.py:30
  111.7 73.6 %copy-start.14 = (bf16[1,1,1536,1536]{3,2,1,0:T(8,128)(2,1)S(1)}, bf16[1,1,1536,1536]{3,2,1,0:T(8,128)(2,1)}, u32[]{:S(2)}) copy-start(bf16[1,1,1536,1536]{3,2,1,0:T(8,128)(2,1)} %all-gather.6.cloned.1.call-done) | copy-start | bytes 14155780
  185.4 2.6 copy-start
  190.1 10.9 %collective-permute-start = (bf16[480,256]{1,0:T(8,128)(2,1)S(1)}, bf16[480,256]{1,0:T(8,128)(2,1)S(1)}, u32[]{:S(2)}, u32[]{:S(2)}) collective-permute-start(bf16[480,256]{1,0:T(8,128)(2,1)S(1)} %select_convert_fusion), channel_id=1, source_target_pairs={{0,16},{16,0},{32,48},{48,32},{64,80},{80,64},{96,112},{112,96},{1... | collective-permute-start | bytes 737288 | tf_op jit(solution)/shard_map/ppermute | solution.py:30
  227.1 25.5 %copy-start.10 = (bf16[96,768]{1,0:T(8,128)(2,1)S(1)}, bf16[96,768]{1,0:T(8,128)(2,1)}, u32[]{:S(2)}) copy-start(bf16[96,768]{1,0:T(8,128)(2,1)} %get-tuple-element.14) | copy-start | bytes 442372
  227.1 25.5 %copy-start.11 = (bf16[96,768]{1,0:T(8,128)(2,1)S(1)}, bf16[96,768]{1,0:T(8,128)(2,1)}, u32[]{:S(2)}) copy-start(bf16[96,768]{1,0:T(8,128)(2,1)} %get-tuple-element.12) | copy-start | bytes 442372
  227.1 25.5 %copy-start.12 = (bf16[96,768]{1,0:T(8,128)(2,1)S(1)}, bf16[96,768]{1,0:T(8,128)(2,1)}, u32[]{:S(2)}) copy-start(bf16[96,768]{1,0:T(8,128)(2,1)} %get-tuple-element.10) | copy-start | bytes 442372
  227.3 25.6 %copy-start.7 = (f32[256,48]{0,1:T(8,128)}, f32[256,48]{0,1:T(8,128)S(1)}, u32[]{:S(2)}) copy-start(f32[256,48]{0,1:T(8,128)S(1)} %fusion.70) | copy-start | bytes 147460
  275.1 23.9 %all-to-all-start.1 = ((bf16[4,16,16,96]{3,2,1,0:T(8,128)(2,1)}), bf16[4,16,16,96]{3,2,1,0:T(8,128)(2,1)S(1)}, u32[]{:S(2)}, u32[]{:S(2)}) async-start(bf16[4,16,16,96]{3,2,1,0:T(8,128)(2,1)} %broadcast_in_dim.70), calls=%async_computation.1 | async-start | bytes 524288 | tf_op jit(solution)/shard_map/all_to_all | solution.py:40
  294.1 106.8 %collective-permute-start.2 = (f32[48,256]{1,0:T(8,128)}, f32[48,256]{1,0:T(8,128)}, u32[]{:S(2)}, u32[]{:S(2)}) collective-permute-start(f32[48,256]{1,0:T(8,128)} %fusion.57), channel_id=1, source_target_pairs={{0,16},{16,0},{32,48},{48,32},{64,80},{80,64},{96,112},{112,96},{1... | collective-permute-start | bytes 147464 | tf_op jit(solution)/shard_map/ppermute | solution.py:30
  304.5 7.9 %copy-start.3 = (bf16[32,384]{1,0:T(8,128)(2,1)}, bf16[32,384]{1,0:T(8,128)(2,1)S(1)}, u32[]{:S(2)}) copy-start(bf16[32,384]{1,0:T(8,128)(2,1)S(1)} %convolution_convert_fusion.1) | copy-start | bytes 73732
  312.4 10.5 %all-to-all-start.2 = ((bf16[8,2,32,96]{3,2,1,0:T(8,128)(2,1)}), bf16[8,2,32,96]{3,2,1,0:T(8,128)(2,1)S(1)}, u32[]{:S(2)}, u32[]{:S(2)}) async-start(bf16[8,2,32,96]{3,2,1,0:T(8,128)(2,1)} %bitcast.55), calls=%async_computation.2 | async-start | bytes 262144 | tf_op jit(solution)/shard_map/all_to_all | solution.py:40
  323.6 10.1 %all-to-all-start.3 = ((bf16[8,2,32,96]{3,2,1,0:T(8,128)(2,1)}), bf16[8,2,32,96]{3,2,1,0:T(8,128)(2,1)}, u32[]{:S(2)}, u32[]{:S(2)}) async-start(bf16[8,2,32,96]{3,2,1,0:T(8,128)(2,1)} %broadcast_in_dim.77), calls=%async_computation.3 | async-start | bytes 262144 | tf_op jit(solution)/shard_map/all_to_all | solution.py:40
  330.5 8.5 %copy-start.6 = (bf16[16,32,96]{2,1,0:T(8,128)(2,1)S(1)}, bf16[16,32,96]{2,1,0:T(8,128)(2,1)}, u32[]{:S(2)}) copy-start(bf16[16,32,96]{2,1,0:T(8,128)(2,1)} %get-tuple-element.44) | copy-start | bytes 294916
  339.0 17.4 %copy-start.2 = (f32[32,16,96]{2,0,1:T(8,128)S(1)}, f32[32,16,96]{2,0,1:T(8,128)}, u32[]{:S(2)}) copy-start(f32[32,16,96]{2,0,1:T(8,128)} %fusion) | copy-start | bytes 589828
  341.3 10.4 %all-to-all-start.4 = ((bf16[16,1,32,96]{3,2,1,0:T(8,128)(2,1)}), bf16[16,1,32,96]{3,2,1,0:T(8,128)(2,1)S(1)}, u32[]{:S(2)}, u32[]{:S(2)}) async-start(bf16[16,1,32,96]{3,2,1,0:T(8,128)(2,1)} %fusion.36), calls=%async_computation.4 | async-start | bytes 262144 | tf_op jit(solution)/shard_map/all_to_all | solution.py:40
  352.4 10.2 %all-to-all-start.5 = ((bf16[16,1,32,96]{3,2,1,0:T(8,128)(2,1)}), bf16[16,1,32,96]{3,2,1,0:T(8,128)(2,1)S(1)}, u32[]{:S(2)}, u32[]{:S(2)}) async-start(bf16[16,1,32,96]{3,2,1,0:T(8,128)(2,1)} %broadcast_in_dim.80), calls=%async_computation.5 | async-start | bytes 262144 | tf_op jit(solution)/shard_map/all_to_all | solution.py:40
  358.8 4.7 %copy-start.5 = (bf16[16,32,96]{2,1,0:T(8,128)(2,1)S(1)}, bf16[16,32,96]{2,1,0:T(8,128)(2,1)}, u32[]{:S(2)}) copy-start(bf16[16,32,96]{2,1,0:T(8,128)(2,1)} %get-tuple-element.45) | copy-start | bytes 294916
  365.2 19.5 %copy-start.4 = (bf16[32,384]{1,0:T(8,128)(2,1)S(1)}, bf16[32,384]{1,0:T(8,128)(2,1)}, u32[]{:S(2)}) copy-start(bf16[32,384]{1,0:T(8,128)(2,1)} %copy-done.3) | copy-start | bytes 73732
  366.2 13.1 %all-to-all-start.6 = ((bf16[32,2,768]{2,1,0:T(2,128)(2,1)}), bf16[32,2,768]{2,1,0:T(2,128)(2,1)S(1)}, u32[]{:S(2)}, u32[]{:S(2)}) async-start(bf16[32,2,768]{2,1,0:T(2,128)(2,1)} %reshape.243), calls=%async_computation.6 | async-start | bytes 196608 | tf_op jit(solution)/shard_map/all_to_all | solution.py:40
  380.7 11.5 %all-to-all-start.7 = ((bf16[32,2,768]{2,1,0:T(2,128)(2,1)}), bf16[32,2,768]{2,1,0:T(2,128)(2,1)S(1)}, u32[]{:S(2)}, u32[]{:S(2)}) async-start(bf16[32,2,768]{2,1,0:T(2,128)(2,1)} %reshape.245), calls=%async_computation.7 | async-start | bytes 196608 | tf_op jit(solution)/shard_map/all_to_all | solution.py:40
  393.8 7.2 %copy-start.8 = (f32[256,48]{0,1:T(8,128)S(1)}, f32[256,48]{0,1:T(8,128)}, u32[]{:S(2)}) copy-start(f32[256,48]{0,1:T(8,128)} %copy-done.7) | copy-start | bytes 147460
  395.8 16.4 %all-to-all-start.8 = ((bf16[16,2,720]{2,1,0:T(2,128)(2,1)}), bf16[16,2,720]{2,1,0:T(2,128)(2,1)S(1)}, u32[]{:S(2)}, u32[]{:S(2)}) async-start(bf16[16,2,720]{2,1,0:T(2,128)(2,1)} %reshape.247), calls=%async_computation.8 | async-start | bytes 98304 | tf_op jit(solution)/shard_map/all_to_all | solution.py:207
Sparse Core Ops, SparseCore 0:
  9.4 76.0 all-gather.5
  87.5 117.3 all-gather.7
where the time goes:
time: 422 us; the launch traced here: 421 us
  blocking collectives  144 us (34%)
  waiting for transfers between devices  109 us (26%)
  starting transfers between devices  73.9 us (18%)
  local copies, waits for them, and re-layouts  30 us (7%)
  matrix products  23.1 us (5%)
  other arithmetic  23 us (5%)
  between operations  17.6 us (4%)
    all_gather x1, waiting for transfers between devices, shards(): d_full0 = lax.all_gather(d_own0, 'row', axis=0, tiled=True)  67.4 us
    all_gather x2, blocking collectives, natural1(): pieces = lax.all_gather(block, 'row', axis=0, tiled=False)  49.4 us
    all_to_all x7, starting transfers between devices, leaf_scatter(): lax.all_to_all(pieces, 'leaf', 0, 0, tiled=True, axis_index_groups=leaf_g...  46.5 us
    all_gather x1, blocking collectives, shards(): lax.all_gather(b0[:, :half], 'row', axis=0, tiled=True)  37 us
    all_gather x1, blocking collectives, shards(): lax.all_gather(b0[:, half:], 'row', axis=0, tiled=True)  36.5 us
    all_to_all x7, waiting for transfers between devices, leaf_scatter(): lax.all_to_all(pieces, 'leaf', 0, 0, tiled=True, axis_index_groups=leaf_g...  30.6 us
    ppermute x3, starting transfers between devices, core_swap(): return lax.ppermute(block, 'leaf', [(i, i ^ 1) for i in range(count)])  22.5 us
    all_to_all x1, blocking collectives, shards(): turned = lax.all_to_all(turned, 'row', 0, 0, tiled=True)  20.8 us
  transfers between devices with their start and end apart: 13, of which 10 were waited for; matrix products, arithmetic and copies ran while one was open for 17% of the time, Pallas kernels for 0%

commit v1 on v0

--- a/solution.py
+++ b/solution.py
@@ -1,3 +1,4 @@
+import functools
 import jax
 import jax.numpy as jnp
 from jax import lax
@@ -5,6 +6,37 @@
 
 F32 = jnp.float32
 BF16 = jnp.bfloat16
+
+
+def clear_run(row_data, out_dim):
+    y2 = list(row_data.shape[1:])
+    y2[out_dim] *= row_data.shape[0]
+    return jnp.moveaxis(row_data, 0, out_dim).reshape(y2)
+
+
+def find_slabs(local_x, a_name, at_axis):
+    extent = jax.lax.axis_size(a_name)
+    all_rows = [(c, (c + 1) % extent) for c in range(extent)]
+    inbox = [(dd, tick) for tick, dd in all_rows]
+    current_block, d_next = ([], [])
+    for ii in [*range(extent - 1)]:
+        if ii % 2 == 0:
+            finding = jax.lax.ppermute(
+                current_block[-1] if current_block else local_x, perm=all_rows, axis_name=a_name
+            )
+            current_block.append(finding)
+        else:
+            d_next.append(
+                jax.lax.ppermute(d_next[-1] if d_next else local_x, perm=inbox, axis_name=a_name)
+            )
+    raw_out = jnp.stack([*current_block[::-1], local_x, *d_next], axis=0)
+    s_next = jax.lax.axis_index(a_name)
+    local_next = s_next - len(current_block)
+    raw_out = raw_out[(jnp.arange(extent) - local_next) % extent]
+    return clear_run(raw_out, at_axis)
+
+
+_feed_pieces_all = functools.partial(find_slabs, a_name="row", at_axis=0)
 
 
 def column_start(ancestor, source, width_all):
@@ -77,10 +109,7 @@
     d_full0 = lax.all_gather(d_own0, "row", axis=0, tiled=True)
     b0 = b_all[: heights[0]]
     z0 = jnp.concatenate(
-        [
-            lax.all_gather(b0[:, :half], "row", axis=0, tiled=True),
-            lax.all_gather(b0[:, half:], "row", axis=0, tiled=True),
-        ],
+        [lax.all_gather(b0[:, :half], "row", axis=0, tiled=True), _feed_pieces_all(b0[:, half:])],
         axis=1,
     )
     d_own1 = d_all[starts[1] : starts[2]]

time: 422 us -> 462 us (1.095)
  starting transfers between devices: 73.9 us -> 124 us
  blocking collectives: 144 us -> 107 us
  local copies, waits for them, and re-layouts: 30 us -> 52.8 us
  waiting for transfers between devices: 109 us -> 116 us
  other arithmetic: 23 us -> 16.6 us
    ppermute x0 -> x15, starting transfers between devices: none -> 49.2 us  [the longest x7 31.3 us: find_slabs(): jax.lax.ppermute(d_next[-1] if d_next else local_x, perm=inbox, axis_name...]
    all_gather x1 -> x0, blocking collectives: 36.5 us -> none  [shards(): lax.all_gather(b0[:, half:], 'row', axis=0, tiled=True)]
    unnamed x38 -> x54, local copies, waits for them, and re-layouts: 4.29 us -> 23.9 us
    ppermute x0 -> x15, waiting for transfers between devices: none -> 6.89 us  [the longest x8 6.87 us: find_slabs(): jax.lax.ppermute(current_block[-1] if current_block else local_x, perm=al...]
  transfers between devices with their start and end apart: 13 -> 28, of which waited for: 10 -> 16; matrix products, arithmetic and copies ran while one was open for 17% -> 20% of each run, Pallas kernels for 0% -> 0%
where the time goes in v1:
time: 462 us; the launch traced here: 459 us
  starting transfers between devices  124 us (27%)
  waiting for transfers between devices  116 us (25%)
  blocking collectives  107 us (23%)
  local copies, waits for them, and re-layouts  52.8 us (11%)
  matrix products  24.2 us (5%)
  between operations  17.6 us (4%)
  other arithmetic  16.6 us (4%)
    all_gather x1, waiting for transfers between devices, shards(): d_full0 = lax.all_gather(d_own0, 'row', axis=0, tiled=True)  65.2 us
    all_gather x2, blocking collectives, natural1(): pieces = lax.all_gather(block, 'row', axis=0, tiled=False)  50.6 us
    all_to_all x7, starting transfers between devices, leaf_scatter(): lax.all_to_all(pieces, 'leaf', 0, 0, tiled=True, axis_index_groups=leaf_g...  46.1 us
    all_gather x1, blocking collectives, shards(): lax.all_gather(b0[:, :half], 'row', axis=0, tiled=True)  37.4 us
    all_to_all x7, waiting for transfers between devices, leaf_scatter(): lax.all_to_all(pieces, 'leaf', 0, 0, tiled=True, axis_index_groups=leaf_g...  34.7 us
    ppermute x7, starting transfers between devices, find_slabs(): jax.lax.ppermute(d_next[-1] if d_next else local_x, perm=inbox, axis_name...  31.3 us
    ppermute x3, starting transfers between devices, core_swap(): return lax.ppermute(block, 'leaf', [(i, i ^ 1) for i in range(count)])  24.1 us
    unnamed x54, local copies, waits for them, and re-layouts  23.9 us
  transfers between devices with their start and end apart: 28, of which 16 were waited for; matrix products, arithmetic and copies ran while one was open for 20% of the time, Pallas kernels for 0%

profile of v1, /device:TPU:1, one launch (start us, length us, event | category | flops | bytes accessed | tf_op | source)
XLA Modules:
  0.0 458.8 jit_solution(8008954051516240355)
XLA Ops:
  20.2 65.2 %all-gather.6.cloned.1.call-done = bf16[1,1,1536,1536]{3,2,1,0:T(8,128)(2,1)} async-done(((bf16[1,1,96,1536]{3,2,1,0:T(8,128)(2,1)}), bf16[1,1,1536,1536]{3,2,1,0:T(8,128)(2,1)}) %all-gather.6.cloned.1.call-update) | async-done | bytes 4718608 | tf_op jit(solution)/shard_map/all_gather | solution.py:109
  88.2 3.8 collective-permute-start.8
  98.9 11.4 %collective-permute-start.16 = (bf16[480,768]{1,0:T(8,128)(2,1)}, bf16[480,768]{1,0:T(8,128)(2,1)}, u32[]{:S(2)}, u32[]{:S(2)}) collective-permute-start(bf16[480,768]{1,0:T(8,128)(2,1)} %slice_dynamic-update-slice_fusion), channel_id=1, source_target_pairs={{0,16},{16,0},{32,48},{48,32},{64,80},{80,64},{96,112},{112,96},{1... | collective-permute-start | bytes 2211848 | tf_op jit(solution)/shard_map/ppermute | solution.py:62
  110.3 37.4 %all_gather.22 = bf16[1536,256]{1,0:T(8,128)(2,1)} all-gather(bf16[96,256]{1,0:T(8,128)(2,1)S(1)} %get-tuple-element.42), channel_id=1, replica_groups=mesh['leaf'=32,'row'=16] {'row'}, dimensions={0}, use_global_device_ids=true | all-gather | bytes 835584 | tf_op jit(solution)/shard_map/all_gather | solution.py:112
  148.6 3.5 collective-permute-start.1
  152.8 3.4 collective-permute-done.1
  159.1 4.2 collective-permute-start.9
  166.4 4.6 collective-permute-start.10
  174.0 4.6 collective-permute-start.11
  181.6 4.6 collective-permute-start.12
  189.0 4.9 %collective-permute-start.13 = (bf16[96,256]{1,0:T(8,128)(2,1)}, bf16[96,256]{1,0:T(8,128)(2,1)}, u32[]{:S(2)}, u32[]{:S(2)}) collective-permute-start(bf16[96,256]{1,0:T(8,128)(2,1)} %collective-permute-done.12), channel_id=1, source_target_pairs={{1,0},{2,1},{3,2},{4,3},{5,4},{6,5},{7,6},{8,7},{9,8},{10,9},{11,1... | collective-permute-start | bytes 147464 | tf_op jit(solution)/shard_map/ppermute | solution.py:30
  201.3 4.6 collective-permute-start.14
  228.8 5.4 %convolution_convert_fusion = bf16[1536,512]{1,0:T(8,128)(2,1)S(1)} fusion(bf16[1536,1536]{1,0:T(8,128)(2,1)} %bitcast.268, bf16[1536,256]{1,0:T(8,128)(2,1)} %bitcast.259, bf16[1536,256]{1,0:T(8,128)(2,1)} %all_gather.22), kind=kOutput, calls=%fused_computation.1 | convolution fusion | flops 2419851264 | bytes 7864320 | tf_op jit(solution)/shard_map/dot_general | solution.py:53
  236.4 10.7 %collective-permute-start.15 = (bf16[480,256]{1,0:T(8,128)(2,1)S(1)}, bf16[480,256]{1,0:T(8,128)(2,1)S(1)}, u32[]{:S(2)}, u32[]{:S(2)}) collective-permute-start(bf16[480,256]{1,0:T(8,128)(2,1)S(1)} %select_convert_fusion), channel_id=1, source_target_pairs={{0,16},{16,0},{32,48},{48,32},{64,80},{80,64},{96,112},{112,96},{1... | collective-permute-start | bytes 737288 | tf_op jit(solution)/shard_map/ppermute | solution.py:62
  248.3 24.3 %all-gather.1 = bf16[1536,256]{1,0:T(8,128)(2,1)S(1)} all-gather(bf16[96,256]{1,0:T(8,128)(2,1)S(1)} %slice.488), channel_id=3, replica_groups=mesh['leaf'=32,'row'=16] {'row'}, dimensions={0}, use_global_device_ids=true | all-gather | bytes 835584 | tf_op jit(solution)/shard_map/all_gather | solution.py:158
  273.3 26.2 %all_gather.26 = bf16[16,96,256]{2,1,0:T(8,128)(2,1)S(1)} all-gather(bf16[1,96,256]{2,1,0:T(8,128)(2,1)S(1)} %fusion.61), channel_id=1, replica_groups=mesh['leaf'=32,'row'=16] {'row'}, dimensions={0}, use_global_device_ids=true | all-gather | bytes 835584 | tf_op jit(solution)/shard_map/all_gather | solution.py:158
  301.5 19.0 %all_to_all.45 = bf16[16,16,384]{2,1,0:T(8,128)(2,1)S(1)} all-to-all(bf16[16,16,384]{2,1,0:T(8,128)(2,1)S(1)} %bitcast.261), channel_id=1, replica_groups=mesh['leaf'=32,'row'=16] {'row'}, dimensions={0} | all-to-all | bytes 393216 | tf_op jit(solution)/shard_map/all_to_all | solution.py:182
  321.4 19.1 %all-to-all-start.1 = ((bf16[4,16,16,96]{3,2,1,0:T(8,128)(2,1)}), bf16[4,16,16,96]{3,2,1,0:T(8,128)(2,1)S(1)}, u32[]{:S(2)}, u32[]{:S(2)}) async-start(bf16[4,16,16,96]{3,2,1,0:T(8,128)(2,1)} %broadcast_in_dim.71), calls=%async_computation.1 | async-start | bytes 524288 | tf_op jit(solution)/shard_map/all_to_all | solution.py:72
  356.8 5.3 %all-to-all-start.2 = ((bf16[8,2,32,96]{3,2,1,0:T(8,128)(2,1)}), bf16[8,2,32,96]{3,2,1,0:T(8,128)(2,1)S(1)}, u32[]{:S(2)}, u32[]{:S(2)}) async-start(bf16[8,2,32,96]{3,2,1,0:T(8,128)(2,1)} %bitcast.73), calls=%async_computation.2 | async-start | bytes 262144 | tf_op jit(solution)/shard_map/all_to_all | solution.py:72
  362.2 5.2 %all-to-all-done.2 = bf16[8,2,32,96]{3,2,1,0:T(8,128)(2,1)S(1)} async-done(((bf16[8,2,32,96]{3,2,1,0:T(8,128)(2,1)}), bf16[8,2,32,96]{3,2,1,0:T(8,128)(2,1)S(1)}, u32[]{:S(2)}, u32[]{:S(2)}) %all-to-all-start.2) | async-done | bytes 98336 | tf_op jit(solution)/shard_map/all_to_all | solution.py:72
  368.0 4.1 all-to-all-start.3
  373.6 3.9 all-to-all-done.3
  380.7 4.2 all-to-all-start.4
  385.1 6.0 %all-to-all-done.4 = bf16[16,1,32,96]{3,2,1,0:T(8,128)(2,1)S(1)} async-done(((bf16[16,1,32,96]{3,2,1,0:T(8,128)(2,1)}), bf16[16,1,32,96]{3,2,1,0:T(8,128)(2,1)S(1)}, u32[]{:S(2)}, u32[]{:S(2)}) %all-to-all-start.4) | async-done | bytes 98336 | tf_op jit(solution)/shard_map/all_to_all | solution.py:72
  391.8 4.0 all-to-all-start.5
  397.4 4.5 all-to-all-done.5
  405.5 5.5 %all-to-all-start.6 = ((bf16[32,2,768]{2,1,0:T(2,128)(2,1)}), bf16[32,2,768]{2,1,0:T(2,128)(2,1)S(1)}, u32[]{:S(2)}, u32[]{:S(2)}) async-start(bf16[32,2,768]{2,1,0:T(2,128)(2,1)} %reshape.304), calls=%async_computation.6 | async-start | bytes 196608 | tf_op jit(solution)/shard_map/all_to_all | solution.py:72
  412.1 6.3 %all-to-all-done.6 = bf16[32,2,768]{2,1,0:T(2,128)(2,1)S(1)} async-done(((bf16[32,2,768]{2,1,0:T(2,128)(2,1)}), bf16[32,2,768]{2,1,0:T(2,128)(2,1)S(1)}, u32[]{:S(2)}, u32[]{:S(2)}) %all-to-all-start.6) | async-done | bytes 98336 | tf_op jit(solution)/shard_map/all_to_all | solution.py:72
  419.8 3.9 all-to-all-start.7
  424.6 6.8 %all-to-all-done.7 = bf16[32,2,768]{2,1,0:T(2,128)(2,1)S(1)} async-done(((bf16[32,2,768]{2,1,0:T(2,128)(2,1)}), bf16[32,2,768]{2,1,0:T(2,128)(2,1)S(1)}, u32[]{:S(2)}, u32[]{:S(2)}) %all-to-all-start.7) | async-done | bytes 98336 | tf_op jit(solution)/shard_map/all_to_all | solution.py:72
  434.0 4.8 %all-to-all-start.8 = ((bf16[16,2,720]{2,1,0:T(2,128)(2,1)}), bf16[16,2,720]{2,1,0:T(2,128)(2,1)S(1)}, u32[]{:S(2)}, u32[]{:S(2)}) async-start(bf16[16,2,720]{2,1,0:T(2,128)(2,1)} %reshape.308), calls=%async_computation.8 | async-start | bytes 98304 | tf_op jit(solution)/shard_map/all_to_all | solution.py:236
  441.2 9.1 %all-to-all-done.8 = bf16[16,2,720]{2,1,0:T(2,128)(2,1)S(1)} async-done(((bf16[16,2,720]{2,1,0:T(2,128)(2,1)}), bf16[16,2,720]{2,1,0:T(2,128)(2,1)S(1)}, u32[]{:S(2)}, u32[]{:S(2)}) %all-to-all-start.8) | async-done | bytes 46112 | tf_op jit(solution)/shard_map/all_to_all | solution.py:236
  (200 shorter events, 110.6 us)
Async XLA Ops:
  6.5 85.5 %copy-start = (bf16[1,1,96,12384]{3,2,1,0:T(8,128)(2,1)S(1)}, bf16[1,1,96,12384]{3,2,1,0:T(8,128)(2,1)}, u32[]{:S(2)}) copy-start(bf16[1,1,96,12384]{3,2,1,0:T(8,128)(2,1)} %param.6) | copy-start | bytes 7133188
  6.5 79.0 %copy-start.5 = (bf16[1,1,189,512]{3,2,1,0:T(8,128)(2,1)S(1)}, bf16[1,1,189,512]{3,2,1,0:T(8,128)(2,1)}, u32[]{:S(2)}) copy-start(bf16[1,1,189,512]{3,2,1,0:T(8,128)(2,1)} %param.4) | copy-start | bytes 580612
  6.5 78.9 %all-gather.6.cloned.1.call-start = ((), (), s32[]{:S(2)}) async-start(), calls=%async_computation.9 | async-start | bytes 5013504 | tf_op jit(solution)/shard_map/all_gather | solution.py:109
  8.4 338.8 %all-gather.8.cloned.1.call-start = ((), (), s32[]{:S(2)}) async-start(), calls=%async_computation.10 | async-start | bytes 7938048 | tf_op jit(solution)/shard_map/all_gather | solution.py:141
  10.8 86.8 %copy-start.1 = (bf16[1,1,189,1536]{3,2,1,0:T(8,128)(2,1)S(1)}, bf16[1,1,189,1536]{3,2,1,0:T(8,128)(2,1)}, u32[]{:S(2)}) copy-start(bf16[1,1,189,1536]{3,2,1,0:T(8,128)(2,1)} %param.5) | copy-start | bytes 1741828
  20.2 160.7 %copy-start.15 = (s32[1,1,15]{2,1,0:T(1,128)S(1)}, s32[1,1,15]{2,1,0:T(1,128)}, u32[]{:S(2)}) copy-start(s32[1,1,15]{2,1,0:T(1,128)} %param.7) | copy-start | bytes 184
  85.5 63.0 %collective-permute-start = (bf16[96,256]{1,0:T(8,128)(2,1)S(1)}, bf16[96,256]{1,0:T(8,128)(2,1)S(1)}, u32[]{:S(2)}, u32[]{:S(2)}) collective-permute-start(bf16[96,256]{1,0:T(8,128)(2,1)S(1)} %get-tuple-element.43), channel_id=1, source_target_pairs={{0,1},{1,2},{2,3},{3,4},{4,5},{5,6},{6,7},{7,8},{8,9},{9,10},{10,1... | collective-permute-start | bytes 147464 | tf_op jit(solution)/shard_map/ppermute | solution.py:24
  88.2 70.9 %collective-permute-start.8 = (bf16[96,256]{1,0:T(8,128)(2,1)S(1)}, bf16[96,256]{1,0:T(8,128)(2,1)S(1)}, u32[]{:S(2)}, u32[]{:S(2)}) collective-permute-start(bf16[96,256]{1,0:T(8,128)(2,1)S(1)} %get-tuple-element.43), channel_id=1, source_target_pairs={{1,0},{2,1},{3,2},{4,3},{5,4},{6,5},{7,6},{8,7},{9,8},{10,9},{11,1... | collective-permute-start | bytes 147464 | tf_op jit(solution)/shard_map/ppermute | solution.py:30
  98.9 148.2 %collective-permute-start.16 = (bf16[480,768]{1,0:T(8,128)(2,1)}, bf16[480,768]{1,0:T(8,128)(2,1)}, u32[]{:S(2)}, u32[]{:S(2)}) collective-permute-start(bf16[480,768]{1,0:T(8,128)(2,1)} %slice_dynamic-update-slice_fusion), channel_id=1, source_target_pairs={{0,16},{16,0},{32,48},{48,32},{64,80},{80,64},{96,112},{112,96},{1... | collective-permute-start | bytes 2211848 | tf_op jit(solution)/shard_map/ppermute | solution.py:62
  148.6 7.6 %collective-permute-start.1 = (bf16[96,256]{1,0:T(8,128)(2,1)S(1)}, bf16[96,256]{1,0:T(8,128)(2,1)S(1)}, u32[]{:S(2)}, u32[]{:S(2)}) collective-permute-start(bf16[96,256]{1,0:T(8,128)(2,1)S(1)} %collective-permute-done), channel_id=1, source_target_pairs={{0,1},{1,2},{2,3},{3,4},{4,5},{5,6},{6,7},{7,8},{8,9},{9,10},{10,1... | collective-permute-start | bytes 147464 | tf_op jit(solution)/shard_map/ppermute | solution.py:24
  156.2 7.6 %collective-permute-start.2 = (bf16[96,256]{1,0:T(8,128)(2,1)S(1)}, bf16[96,256]{1,0:T(8,128)(2,1)S(1)}, u32[]{:S(2)}, u32[]{:S(2)}) collective-permute-start(bf16[96,256]{1,0:T(8,128)(2,1)S(1)} %collective-permute-done.1), channel_id=1, source_target_pairs={{0,1},{1,2},{2,3},{3,4},{4,5},{5,6},{6,7},{7,8},{8,9},{9,10},{10,1... | collective-permute-start | bytes 147464 | tf_op jit(solution)/shard_map/ppermute | solution.py:24
  159.1 7.3 %collective-permute-start.9 = (bf16[96,256]{1,0:T(8,128)(2,1)S(1)}, bf16[96,256]{1,0:T(8,128)(2,1)S(1)}, u32[]{:S(2)}, u32[]{:S(2)}) collective-permute-start(bf16[96,256]{1,0:T(8,128)(2,1)S(1)} %collective-permute-done.8), channel_id=1, source_target_pairs={{1,0},{2,1},{3,2},{4,3},{5,4},{6,5},{7,6},{8,7},{9,8},{10,9},{11,1... | collective-permute-start | bytes 147464 | tf_op jit(solution)/shard_map/ppermute | solution.py:30
  163.8 7.6 %collective-permute-start.3 = (bf16[96,256]{1,0:T(8,128)(2,1)S(1)}, bf16[96,256]{1,0:T(8,128)(2,1)S(1)}, u32[]{:S(2)}, u32[]{:S(2)}) collective-permute-start(bf16[96,256]{1,0:T(8,128)(2,1)S(1)} %collective-permute-done.2), channel_id=1, source_target_pairs={{0,1},{1,2},{2,3},{3,4},{4,5},{5,6},{6,7},{7,8},{8,9},{9,10},{10,1... | collective-permute-start | bytes 147464 | tf_op jit(solution)/shard_map/ppermute | solution.py:24
  166.4 7.6 %collective-permute-start.10 = (bf16[96,256]{1,0:T(8,128)(2,1)S(1)}, bf16[96,256]{1,0:T(8,128)(2,1)}, u32[]{:S(2)}, u32[]{:S(2)}) collective-permute-start(bf16[96,256]{1,0:T(8,128)(2,1)S(1)} %collective-permute-done.9), channel_id=1, source_target_pairs={{1,0},{2,1},{3,2},{4,3},{5,4},{6,5},{7,6},{8,7},{9,8},{10,9},{11,1... | collective-permute-start | bytes 147464 | tf_op jit(solution)/shard_map/ppermute | solution.py:30
  171.4 7.6 %collective-permute-start.4 = (bf16[96,256]{1,0:T(8,128)(2,1)S(1)}, bf16[96,256]{1,0:T(8,128)(2,1)}, u32[]{:S(2)}, u32[]{:S(2)}) collective-permute-start(bf16[96,256]{1,0:T(8,128)(2,1)S(1)} %collective-permute-done.3), channel_id=1, source_target_pairs={{0,1},{1,2},{2,3},{3,4},{4,5},{5,6},{6,7},{7,8},{8,9},{9,10},{10,1... | collective-permute-start | bytes 147464 | tf_op jit(solution)/shard_map/ppermute | solution.py:24
  174.0 7.6 %collective-permute-start.11 = (bf16[96,256]{1,0:T(8,128)(2,1)}, bf16[96,256]{1,0:T(8,128)(2,1)}, u32[]{:S(2)}, u32[]{:S(2)}) collective-permute-start(bf16[96,256]{1,0:T(8,128)(2,1)} %collective-permute-done.10), channel_id=1, source_target_pairs={{1,0},{2,1},{3,2},{4,3},{5,4},{6,5},{7,6},{8,7},{9,8},{10,9},{11,1... | collective-permute-start | bytes 147464 | tf_op jit(solution)/shard_map/ppermute | solution.py:30
  179.0 8.1 %collective-permute-start.5 = (bf16[96,256]{1,0:T(8,128)(2,1)}, bf16[96,256]{1,0:T(8,128)(2,1)}, u32[]{:S(2)}, u32[]{:S(2)}) collective-permute-start(bf16[96,256]{1,0:T(8,128)(2,1)} %collective-permute-done.4), channel_id=1, source_target_pairs={{0,1},{1,2},{2,3},{3,4},{4,5},{5,6},{6,7},{7,8},{8,9},{9,10},{10,1... | collective-permute-start | bytes 147464 | tf_op jit(solution)/shard_map/ppermute | solution.py:24
  181.6 7.4 %collective-permute-start.12 = (bf16[96,256]{1,0:T(8,128)(2,1)}, bf16[96,256]{1,0:T(8,128)(2,1)}, u32[]{:S(2)}, u32[]{:S(2)}) collective-permute-start(bf16[96,256]{1,0:T(8,128)(2,1)} %collective-permute-done.11), channel_id=1, source_target_pairs={{1,0},{2,1},{3,2},{4,3},{5,4},{6,5},{7,6},{8,7},{9,8},{10,9},{11,1... | collective-permute-start | bytes 147464 | tf_op jit(solution)/shard_map/ppermute | solution.py:30
  187.1 8.3 %collective-permute-start.6 = (bf16[96,256]{1,0:T(8,128)(2,1)}, bf16[96,256]{1,0:T(8,128)(2,1)}, u32[]{:S(2)}, u32[]{:S(2)}) collective-permute-start(bf16[96,256]{1,0:T(8,128)(2,1)} %collective-permute-done.5), channel_id=1, source_target_pairs={{0,1},{1,2},{2,3},{3,4},{4,5},{5,6},{6,7},{7,8},{8,9},{9,10},{10,1... | collective-permute-start | bytes 147464 | tf_op jit(solution)/shard_map/ppermute | solution.py:24
  189.0 12.3 %collective-permute-start.13 = (bf16[96,256]{1,0:T(8,128)(2,1)}, bf16[96,256]{1,0:T(8,128)(2,1)}, u32[]{:S(2)}, u32[]{:S(2)}) collective-permute-start(bf16[96,256]{1,0:T(8,128)(2,1)} %collective-permute-done.12), channel_id=1, source_target_pairs={{1,0},{2,1},{3,2},{4,3},{5,4},{6,5},{7,6},{8,7},{9,8},{10,9},{11,1... | collective-permute-start | bytes 147464 | tf_op jit(solution)/shard_map/ppermute | solution.py:30
  195.4 10.5 %collective-permute-start.7 = (bf16[96,256]{1,0:T(8,128)(2,1)}, bf16[96,256]{1,0:T(8,128)(2,1)}, u32[]{:S(2)}, u32[]{:S(2)}) collective-permute-start(bf16[96,256]{1,0:T(8,128)(2,1)} %collective-permute-done.6), channel_id=1, source_target_pairs={{0,1},{1,2},{2,3},{3,4},{4,5},{5,6},{6,7},{7,8},{8,9},{9,10},{10,1... | collective-permute-start | bytes 147464 | tf_op jit(solution)/shard_map/ppermute | solution.py:24
  201.3 24.3 %collective-permute-start.14 = (bf16[96,256]{1,0:T(8,128)(2,1)}, bf16[96,256]{1,0:T(8,128)(2,1)S(1)}, u32[]{:S(2)}, u32[]{:S(2)}) collective-permute-start(bf16[96,256]{1,0:T(8,128)(2,1)} %collective-permute-done.13), channel_id=1, source_target_pairs={{1,0},{2,1},{3,2},{4,3},{5,4},{6,5},{7,6},{8,7},{9,8},{10,9},{11,1... | collective-permute-start | bytes 147464 | tf_op jit(solution)/shard_map/ppermute | solution.py:30
  236.4 11.8 %collective-permute-start.15 = (bf16[480,256]{1,0:T(8,128)(2,1)S(1)}, bf16[480,256]{1,0:T(8,128)(2,1)S(1)}, u32[]{:S(2)}, u32[]{:S(2)}) collective-permute-start(bf16[480,256]{1,0:T(8,128)(2,1)S(1)} %select_convert_fusion), channel_id=1, source_target_pairs={{0,16},{16,0},{32,48},{48,32},{64,80},{80,64},{96,112},{112,96},{1... | collective-permute-start | bytes 737288 | tf_op jit(solution)/shard_map/ppermute | solution.py:62
  321.4 24.2 %all-to-all-start.1 = ((bf16[4,16,16,96]{3,2,1,0:T(8,128)(2,1)}), bf16[4,16,16,96]{3,2,1,0:T(8,128)(2,1)S(1)}, u32[]{:S(2)}, u32[]{:S(2)}) async-start(bf16[4,16,16,96]{3,2,1,0:T(8,128)(2,1)} %broadcast_in_dim.71), calls=%async_computation.1 | async-start | bytes 524288 | tf_op jit(solution)/shard_map/all_to_all | solution.py:72
  340.7 99.6 %collective-permute-start.17 = (f32[48,256]{1,0:T(8,128)S(1)}, f32[48,256]{1,0:T(8,128)}, u32[]{:S(2)}, u32[]{:S(2)}) collective-permute-start(f32[48,256]{1,0:T(8,128)S(1)} %fusion.57), channel_id=1, source_target_pairs={{0,16},{16,0},{32,48},{48,32},{64,80},{80,64},{96,112},{112,96},{1... | collective-permute-start | bytes 147464 | tf_op jit(solution)/shard_map/ppermute | solution.py:62
  356.8 10.5 %all-to-all-start.2 = ((bf16[8,2,32,96]{3,2,1,0:T(8,128)(2,1)}), bf16[8,2,32,96]{3,2,1,0:T(8,128)(2,1)S(1)}, u32[]{:S(2)}, u32[]{:S(2)}) async-start(bf16[8,2,32,96]{3,2,1,0:T(8,128)(2,1)} %bitcast.73), calls=%async_computation.2 | async-start | bytes 262144 | tf_op jit(solution)/shard_map/all_to_all | solution.py:72
  368.0 9.4 %all-to-all-start.3 = ((bf16[8,2,32,96]{3,2,1,0:T(8,128)(2,1)}), bf16[8,2,32,96]{3,2,1,0:T(8,128)(2,1)S(1)}, u32[]{:S(2)}, u32[]{:S(2)}) async-start(bf16[8,2,32,96]{3,2,1,0:T(8,128)(2,1)} %broadcast_in_dim.78), calls=%async_computation.3 | async-start | bytes 262144 | tf_op jit(solution)/shard_map/all_to_all | solution.py:72
  380.7 10.4 %all-to-all-start.4 = ((bf16[16,1,32,96]{3,2,1,0:T(8,128)(2,1)}), bf16[16,1,32,96]{3,2,1,0:T(8,128)(2,1)S(1)}, u32[]{:S(2)}, u32[]{:S(2)}) async-start(bf16[16,1,32,96]{3,2,1,0:T(8,128)(2,1)} %fusion.36), calls=%async_computation.4 | async-start | bytes 262144 | tf_op jit(solution)/shard_map/all_to_all | solution.py:72
  391.8 10.2 %all-to-all-start.5 = ((bf16[16,1,32,96]{3,2,1,0:T(8,128)(2,1)}), bf16[16,1,32,96]{3,2,1,0:T(8,128)(2,1)S(1)}, u32[]{:S(2)}, u32[]{:S(2)}) async-start(bf16[16,1,32,96]{3,2,1,0:T(8,128)(2,1)} %broadcast_in_dim.81), calls=%async_computation.5 | async-start | bytes 262144 | tf_op jit(solution)/shard_map/all_to_all | solution.py:72
  405.5 13.0 %all-to-all-start.6 = ((bf16[32,2,768]{2,1,0:T(2,128)(2,1)}), bf16[32,2,768]{2,1,0:T(2,128)(2,1)S(1)}, u32[]{:S(2)}, u32[]{:S(2)}) async-start(bf16[32,2,768]{2,1,0:T(2,128)(2,1)} %reshape.304), calls=%async_computation.6 | async-start | bytes 196608 | tf_op jit(solution)/shard_map/all_to_all | solution.py:72
  419.8 11.5 %all-to-all-start.7 = ((bf16[32,2,768]{2,1,0:T(2,128)(2,1)}), bf16[32,2,768]{2,1,0:T(2,128)(2,1)S(1)}, u32[]{:S(2)}, u32[]{:S(2)}) async-start(bf16[32,2,768]{2,1,0:T(2,128)(2,1)} %reshape.306), calls=%async_computation.7 | async-start | bytes 196608 | tf_op jit(solution)/shard_map/all_to_all | solution.py:72
  434.0 16.4 %all-to-all-start.8 = ((bf16[16,2,720]{2,1,0:T(2,128)(2,1)}), bf16[16,2,720]{2,1,0:T(2,128)(2,1)S(1)}, u32[]{:S(2)}, u32[]{:S(2)}) async-start(bf16[16,2,720]{2,1,0:T(2,128)(2,1)} %reshape.308), calls=%async_computation.8 | async-start | bytes 98304 | tf_op jit(solution)/shard_map/all_to_all | solution.py:236
  (12 other events, 324.0 us)
Sparse Core Ops, SparseCore 0:
  9.4 76.0 all-gather.5
  87.5 115.0 all-gather.7
